TPU v7x, 32 devices: a whole 2x2x4 slice. The times are simulated.
32 devices in a mesh: ctx: 8 (over z, x), tp: 4 (over y, core).
Axes of the slice: x: 2, y: 2, z: 4, core: 2. Of those that a mesh axis runs over, the one named last changes fastest.
Arguments:
- queries: bfloat16 [2048, 2560], P('ctx', 'tp'), may hold values from -5 to 5
- keys: bfloat16 [2048, 2560], P('ctx', 'tp'), may hold values from -5 to 5
- values: bfloat16 [2048, 2560], P('ctx', 'tp'), may hold values from -6 to 6
- block_mask: int32 [16, 16], replicated, may hold values from 0 to 1, as said below
- w_out: bfloat16 [2560, 5120], P('tp'), may hold values from -0.125 to 0.125
Outputs:
- mixed: bfloat16 [2048, 5120], P('ctx', 'tp')
Inputs may be any that keep to these rules, and one draw needn't show every extreme that they name: block_mask[b, b] = 1 for every block b. block_mask[i, j] = 0 whenever the ctx indices i // 2 and j // 2 differ by more than 2; where they differ by exactly 2 and i and j have the same position within their devices, block_mask[i, j] = 1.
All inputs are finite; a program needn't handle non-finite values.
Results may differ from a plain program's by a relative error of at most 0.014.
Values may be sent and summed in bfloat16 or wider, within the bound.
A program may use at most 64 MiB of HBM per device.

v0:
```python
import functools
import math

import jax
import jax.numpy as jnp
from jax import lax
from jax.experimental import pallas as pl
from jax.experimental.pallas import tpu as pltpu
from jax.sharding import PartitionSpec as P

HD = 128
BLK = 128
MESH = pl.DeviceIdType.MESH
K, V = 0, 1
OUTER_FIRST, ROW_FIRST = 0, 1


def kernel(
    reach, count, tp_count, chunks,
    mask_ref, q_ref, k_ref, v_ref, w_ref, near_ref, far_ref,
    kv, w_vm, acc, peak, att, stage_p, recv_p, stage_y, final,
    kv_local, w_local, own_send, relay_send, kv_recv, p_send, p_recv, y_send, y_recv, near_sem,
):
    tok, cols = q_ref.shape
    heads = cols // HD
    per = tok // BLK
    chips = tp_count // 2
    out_cols = near_ref.shape[1]
    width = out_cols // chunks
    ctx = lax.axis_index("ctx")
    t = lax.axis_index("tp")
    inner = lax.rem(ctx, reach)
    core = lax.rem(t, 2)
    chip = t // 2
    partner = chip * 2 + 1 - core

    def tp_of(jy, which):
        return lax.rem(chip + jy, chips) * 2 + which

    def each_peer(fn):
        if reach == 2:
            fn(1)
        elif reach > 2:
            def step(j, carry):
                fn(j)
                return carry
            lax.fori_loop(1, reach, step, 0)

    def row_peer(j):
        return ctx - inner + lax.rem(inner + j, reach)

    def inside(c):
        return jnp.logical_and(c >= 0, c < count)

    part_rows = tok // 2

    def part_of(half, kind):
        return (k_ref, v_ref)[kind].at[half * part_rows:(half + 1) * part_rows, :]

    own = [
        pltpu.make_async_copy(
            part_of(half, kind), kv.at[reach, half * 2 + kind], kv_local.at[half * 2 + kind]
        )
        for half in (0, 1) for kind in (K, V)
    ]
    weights = [
        pltpu.make_async_copy(
            w_ref.at[:, s * out_cols:(s + 1) * out_cols], w_vm.at[s], w_local.at[s]
        )
        for s in range(tp_count)
    ]
    for copy in own:
        copy.start()

    barrier = pltpu.get_barrier_semaphore()

    def greet(c, tt):
        pl.semaphore_signal(barrier, inc=1, device_id=(c, tt), device_id_type=MESH)

    each_peer(lambda j: greet(row_peer(j), t))
    for away in (-reach, reach):
        @pl.when(inside(ctx + away))
        def _(away=away):
            greet(ctx + away, t)
    greet(ctx, partner)
    for jy in range(1, chips):
        greet(ctx, tp_of(jy, core))
    outer_count = inside(ctx - reach).astype(jnp.int32) + inside(ctx + reach).astype(jnp.int32)
    pl.semaphore_wait(barrier, reach - 1 + 1 + chips - 1 + outer_count)

    class Pair:
        def __init__(self, make):
            self.copies = [make(K), make(V)]

        def start(self):
            for copy in self.copies:
                copy.start()

        def wait_send(self):
            for copy in self.copies:
                copy.wait_send()

        def wait_recv(self):
            for copy in self.copies:
                copy.wait_recv()

    def own_copy(dest, half):
        return Pair(lambda kind: pltpu.make_async_remote_copy(
            src_ref=part_of(half, kind),
            dst_ref=kv.at[ctx - dest + reach, half * 2 + kind],
            send_sem=own_send.at[dest - ctx + reach, half * 2 + kind],
            recv_sem=kv_recv.at[ctx - dest + reach, half * 2 + kind],
            device_id=(dest, t),
            device_id_type=MESH,
        ))

    def outer(fn):
        for away in (-reach, reach):
            @pl.when(inside(ctx + away))
            def _(away=away):
                fn(ctx + away)

    each_peer(lambda j: own_copy(row_peer(j), ROW_FIRST).start())
    outer(lambda dest: own_copy(dest, OUTER_FIRST).start())
    each_peer(lambda j: own_copy(row_peer(j), OUTER_FIRST).start())
    outer(lambda dest: own_copy(dest, ROW_FIRST).start())
    for copy in weights:
        copy.start()

    def wait_piece(src, half):
        slot = src - ctx + reach
        Pair(lambda kind: pltpu.make_async_remote_copy(
            src_ref=kv.at[slot, half * 2 + kind],
            dst_ref=kv.at[slot, half * 2 + kind],
            send_sem=own_send.at[slot, half * 2 + kind],
            recv_sem=kv_recv.at[slot, half * 2 + kind],
            device_id=(ctx, partner),
            device_id_type=MESH,
        )).wait_recv()

    def attend(src, halves, first=False):
        slot = src - ctx + reach
        factor = jnp.float32(HD ** (-0.5) * math.log2(math.e))
        half_blocks = per // 2
        blocks = [half * half_blocks + b for half in halves for b in range(half_blocks)]
        span = len(blocks) * BLK
        bias_rows = []
        for a in range(per):
            parts = []
            for b in blocks:
                flag = mask_ref[ctx * per + a, src * per + b]
                value = jnp.where(flag > 0, jnp.float32(0.0), jnp.float32(-1e30))
                parts.append(jnp.full((1, BLK), value, jnp.float32))
            bias_rows.append(jnp.concatenate(parts, axis=1))
        ones = jnp.ones((span, HD), jnp.bfloat16)
        for h in range(heads):
            lanes = slice(h * HD, (h + 1) * HD)
            key = jnp.concatenate([kv[slot, half * 2 + K, :, lanes] for half in halves], axis=0)
            value = jnp.concatenate([kv[slot, half * 2 + V, :, lanes] for half in halves], axis=0)
            raw = lax.dot_general(
                q_ref[:, lanes], key, (((1,), (1,)), ((), ())),
                preferred_element_type=jnp.float32,
            )
            weights_of, fades = [], []
            for a in range(per):
                rows = slice(a * BLK, (a + 1) * BLK)
                scores = raw[rows] + bias_rows[a]
                top = jnp.broadcast_to(jnp.max(scores, axis=1, keepdims=True), (BLK, HD))
                if not first:
                    before = peak[h, rows, :]
                    top = jnp.maximum(before, top)
                    fades.append(jnp.exp2((before - top) * factor))
                peak[h, rows, :] = top
                wide_top = jnp.concatenate([top] * len(blocks), axis=1)
                weights_of.append(jnp.exp2((scores - wide_top) * factor).astype(jnp.bfloat16))
            product = jnp.dot(
                jnp.concatenate(weights_of, axis=0),
                jnp.concatenate([value, ones], axis=1),
                preferred_element_type=jnp.float32,
            )
            if not first:
                fade = jnp.concatenate(fades, axis=0)
                product = product + acc[h] * jnp.concatenate([fade, fade], axis=1)
            acc[h] = product

    for copy in own:
        copy.wait()
    attend(ctx, (0, 1), True)

    def row_first_relay(j):
        peer = row_peer(j)
        dest = jnp.where(peer > ctx, ctx + reach, ctx - reach)
        return inside(dest), Pair(lambda kind: pltpu.make_async_remote_copy(
            src_ref=kv.at[peer - ctx + reach, ROW_FIRST * 2 + kind],
            dst_ref=kv.at[peer - dest + reach, ROW_FIRST * 2 + kind],
            send_sem=relay_send.at[peer - ctx + reach, ROW_FIRST * 2 + kind],
            recv_sem=kv_recv.at[peer - dest + reach, ROW_FIRST * 2 + kind],
            device_id=(dest, t),
            device_id_type=MESH,
        ))

    def outer_first_relay(j):
        peer = row_peer(j)
        src = jnp.where(peer < ctx, ctx - reach, ctx + reach)
        return inside(src), Pair(lambda kind: pltpu.make_async_remote_copy(
            src_ref=kv.at[src - ctx + reach, OUTER_FIRST * 2 + kind],
            dst_ref=kv.at[src - peer + reach, OUTER_FIRST * 2 + kind],
            send_sem=relay_send.at[peer - ctx + reach, OUTER_FIRST * 2 + kind],
            recv_sem=kv_recv.at[src - peer + reach, OUTER_FIRST * 2 + kind],
            device_id=(peer, t),
            device_id_type=MESH,
        ))

    def start_relay(make, j):
        valid, copy = make(j)

        @pl.when(valid)
        def _():
            copy.start()

    def end_relay(make, j):
        valid, copy = make(j)

        @pl.when(valid)
        def _():
            copy.wait_send()

    def pass_row(j):
        wait_piece(row_peer(j), ROW_FIRST)
        start_relay(row_first_relay, j)

    each_peer(pass_row)
    outer(lambda src: wait_piece(src, OUTER_FIRST))
    each_peer(lambda j: start_relay(outer_first_relay, j))
    each_peer(lambda j: attend(row_peer(j), (ROW_FIRST,)))
    outer(lambda src: attend(src, (OUTER_FIRST,)))

    def take_row(j):
        wait_piece(row_peer(j), OUTER_FIRST)
        attend(row_peer(j), (OUTER_FIRST,))

    each_peer(take_row)

    def take_outer(src):
        wait_piece(src, ROW_FIRST)
        attend(src, (ROW_FIRST,))

    outer(take_outer)
    for copy in weights:
        copy.wait()

    def take_diagonal(j):
        peer = row_peer(j)
        src = jnp.where(peer > ctx, peer - reach, peer + reach)

        @pl.when(inside(src))
        def _():
            wait_piece(src, OUTER_FIRST)
            wait_piece(src, ROW_FIRST)
            attend(src, (0, 1))

    each_peer(take_diagonal)

    for h in range(heads):
        lanes = slice(h * HD, (h + 1) * HD)
        att[:, lanes] = (acc[h, :, :HD] * (1.0 / acc[h, :, HD:])).astype(jnp.bfloat16)

    def project(slab, k):
        return jnp.dot(
            att[...], w_vm[slab, :, k * width:(k + 1) * width],
            preferred_element_type=jnp.float32,
        )

    def partner_copy(jy, k):
        return pltpu.make_async_remote_copy(
            src_ref=stage_p.at[jy, k],
            dst_ref=recv_p.at[jy, k],
            send_sem=p_send.at[jy, k],
            recv_sem=p_recv.at[jy, k],
            device_id=(ctx, partner),
            device_id_type=MESH,
        )

    def chip_copy(jy, k):
        return pltpu.make_async_remote_copy(
            src_ref=stage_y.at[jy, k],
            dst_ref=far_ref.at[chips - jy - 1, :, k * width:(k + 1) * width],
            send_sem=y_send.at[jy, k],
            recv_sem=y_recv.at[chips - jy, k],
            device_id=(ctx, tp_of(jy, core)),
            device_id_type=MESH,
        )

    def near_copy(k):
        return pltpu.make_async_copy(
            final.at[k], near_ref.at[:, k * width:(k + 1) * width], near_sem.at[k]
        )

    pending = []

    def push(copy):
        while pending:
            pending.pop().start()
        if copy is not None:
            pending.append(copy)

    for jy in range(1, chips):
        there, here = tp_of(jy, 1 - core), tp_of(jy, core)
        for step in range(chunks + 1):
            if step < chunks:
                @pl.when(t >= 0)
                def _():
                    stage_p[jy, step] = project(there, step).astype(jnp.bfloat16)
                push(partner_copy(jy, step))
            if step > 0:
                k = step - 1
                if step == chunks:
                    push(None)
                partner_copy(jy, k).wait_recv()

                @pl.when(t >= 0)
                def _():
                    mine = project(here, k) + recv_p[jy, k].astype(jnp.float32)
                    stage_y[jy, k] = mine.astype(jnp.bfloat16)
                push(chip_copy(jy, k))
    for k in range(chunks):
        stage_p[0, k] = project(tp_of(0, 1 - core), k).astype(jnp.bfloat16)
        push(partner_copy(0, k))
    for k in range(chunks):
        mine = project(tp_of(0, core), k)
        push(None)
        partner_copy(0, k).wait_recv()
        final[k] = mine + recv_p[0, k].astype(jnp.float32)
        push(near_copy(k))
    push(None)
    for k in range(chunks):
        for jy in range(1, chips):
            chip_copy(chips - jy, k).wait_recv()
        near_copy(k).wait()

    each_peer(lambda j: own_copy(row_peer(j), ROW_FIRST).wait_send())
    each_peer(lambda j: own_copy(row_peer(j), OUTER_FIRST).wait_send())
    outer(lambda dest: own_copy(dest, OUTER_FIRST).wait_send())
    outer(lambda dest: own_copy(dest, ROW_FIRST).wait_send())
    each_peer(lambda j: end_relay(row_first_relay, j))
    each_peer(lambda j: end_relay(outer_first_relay, j))
    for jy in range(chips):
        for k in range(chunks):
            partner_copy(jy, k).wait_send()
    for jy in range(1, chips):
        for k in range(chunks):
            chip_copy(jy, k).wait_send()


def shards(count, tp_count, queries, keys, values, block_mask, w_out):
    tok, cols = queries.shape
    heads = cols // HD
    reach = count // 4
    chips = tp_count // 2
    depth, wide = w_out.shape
    out_cols = wide // tp_count
    chunks = max(1, out_cols // 256)
    width = out_cols // chunks
    bf16, f32 = jnp.bfloat16, jnp.float32
    dma = pltpu.SemaphoreType.DMA
    slots = 2 * reach + 1
    near, far = pl.pallas_call(
        functools.partial(kernel, reach, count, tp_count, chunks),
        out_shape=[
            jax.ShapeDtypeStruct((tok, out_cols), f32),
            jax.ShapeDtypeStruct((chips - 1, tok, out_cols), bf16),
        ],
        in_specs=[
            pl.BlockSpec(memory_space=pltpu.SMEM),
            pl.BlockSpec(memory_space=pltpu.VMEM),
            pl.BlockSpec(memory_space=pl.ANY),
            pl.BlockSpec(memory_space=pl.ANY),
            pl.BlockSpec(memory_space=pl.ANY),
        ],
        out_specs=[pl.BlockSpec(memory_space=pl.ANY)] * 2,
        scratch_shapes=[
            pltpu.VMEM((slots, 4, tok // 2, cols), bf16),
            pltpu.VMEM((tp_count, depth, out_cols), bf16),
            pltpu.VMEM((heads, tok, 2 * HD), f32),
            pltpu.VMEM((heads, tok, HD), f32),
            pltpu.VMEM((tok, cols), bf16),
            pltpu.VMEM((chips, chunks, tok, width), bf16),
            pltpu.VMEM((chips, chunks, tok, width), bf16),
            pltpu.VMEM((chips, chunks, tok, width), bf16),
            pltpu.VMEM((chunks, tok, width), f32),
            dma((4,)),
            dma((tp_count,)),
            dma((slots, 4)),
            dma((slots, 4)),
            dma((slots, 4)),
            dma((chips, chunks)),
            dma((chips, chunks)),
            dma((chips, chunks)),
            dma((chips, chunks)),
            dma((chunks,)),
        ],
        compiler_params=pltpu.CompilerParams(
            collective_id=0, has_side_effects=True, vmem_limit_bytes=60 * 1024 * 1024
        ),
    )(block_mask, queries, keys, values, w_out)
    for other in range(chips - 1):
        near = near + far[other].astype(f32)
    return near.astype(bf16)


def solution(mesh):
    return jax.shard_map(
        functools.partial(shards, mesh.shape["ctx"], mesh.shape["tp"]),
        mesh=mesh,
        in_specs=(P("ctx", "tp"), P("ctx", "tp"), P("ctx", "tp"), P(), P("tp", None)),
        out_specs=P("ctx", "tp"),
        check_vma=False,
    )
```

profile of v0, /device:TPU:11, one launch (start us, length us, event | category | flops | bytes accessed | tf_op | source)
XLA Modules:
  0.0 48.3 jit_solution(12919618478712842129)
XLA Ops:
  0.0 45.8 %shard_map.55 = (f32[256,1280]{1,0:T(8,128)}, bf16[1,256,1280]{2,1,0:T(8,128)(2,1)}) custom-call(s32[16,16]{1,0:T(8,128)} %mask_ref.1, bf16[256,640]{1,0:T(8,128)(2,1)} %q_ref.1, bf16[256,640]{1,0:T(8,128)(2,1)} %k_ref.1, bf16[256,640]{1,0:T(8,128)(2,1)} %v_ref.1, bf16[640,5120]{1,0:T(8,128)(2,1)} %w_ref.1), custom_call_target="tpu_custom_call" | custom-call | tf_op jit(solution)/shard_map/pallas_call | solution.py:367
  45.8 2.4 %fusion = bf16[256,1280]{1,0:T(8,128)(2,1)} fusion(f32[256,1280]{1,0:T(8,128)} %get-tuple-element.7, bf16[1,256,1280]{2,1,0:T(8,128)(2,1)} %get-tuple-element.8), kind=kLoop, calls=%fused_computation.1 | loop fusion | flops 983040 | bytes 2621440 | tf_op jit(solution)/shard_map/convert_element_type | solution.py:408
where the time goes:
time: 48.5 us; the launch traced here: 48.3 us
  Pallas kernels  45.8 us (94%)
  other arithmetic  2.43 us (5%)
    pallas_call x1, Pallas kernels, shards(): pl.pallas_call(functools.partial(kernel, reach, count, tp_count, chunks),...  45.8 us
    convert_element_type x1, other arithmetic, shards(): return near.astype(bf16)  2.43 us

commit v1 on v0

v1 whole, which is shorter than its diff:
```python
import functools
import math

import jax
import jax.numpy as jnp
from jax import lax
from jax.experimental import pallas as pl
from jax.experimental.pallas import tpu as pltpu
from jax.sharding import PartitionSpec as P

HD = 128
BLK = 128
MESH = pl.DeviceIdType.MESH
K, V = 0, 1
DOWN, UP = 0, 1
NONE = -1e30


def kernel(
    reach, count, tp_count, chunks,
    mask_ref, q_ref, k_ref, v_ref, w_ref, out_ref,
    q_own, kv_row, kv_col, q_row, q_col, o_row, o_col, got_row, got_col,
    lse_row, lse_col, got_lse_row, got_lse_col, acc, peak, att, att_peer,
    w_own, w_peer, stage_y, recv_y, near, final,
    own_sem, w_sem, wp_send, wp_recv, kvr_send, kvr_recv, kvc_send, kvc_recv,
    qr_send, qr_recv, qc_send, qc_recv, or_send, or_recv, oc_send, oc_recv,
    lr_send, lr_recv, lc_send, lc_recv, att_send, att_recv, y_send, y_recv, out_sem,
):
    tok, cols = q_own.shape
    heads = cols // HD
    per = tok // BLK
    chips = tp_count // 2
    out_cols = out_ref.shape[1]
    width = out_cols // chunks
    half = heads // 2
    odd = heads % 2
    middle = half
    ctx = lax.axis_index("ctx")
    t = lax.axis_index("tp")
    inner = lax.rem(ctx, reach)
    core = lax.rem(t, 2)
    chip = t // 2
    partner = chip * 2 + 1 - core
    factor = jnp.float32(HD ** (-0.5) * math.log2(math.e))

    def tp_of(jy, which):
        return lax.rem(chip + jy, chips) * 2 + which

    def each_peer(fn):
        if reach == 2:
            fn(1 - inner)
        elif reach > 2:
            def step(j, carry):
                fn(lax.rem(inner + j, reach))
                return carry
            lax.fori_loop(1, reach, step, 0)

    def in_row(p):
        return ctx - inner + p

    def outer_of(d):
        return ctx + (2 * d - 1) * reach

    def inside(c):
        return jnp.logical_and(c >= 0, c < count)

    def each_outer(fn):
        for d in (DOWN, UP):
            @pl.when(inside(outer_of(d)))
            def _(d=d):
                fn(d)

    def lanes(h):
        return slice(h * HD, (h + 1) * HD)

    def rows(r):
        return slice(r * BLK, (r + 1) * BLK)

    def remote(src, dst, send, recv, c, tt):
        return pltpu.make_async_remote_copy(
            src_ref=src, dst_ref=dst, send_sem=send, recv_sem=recv,
            device_id=(c, tt), device_id_type=MESH,
        )

    def kv_row_copy(p, kind, h, slot=None):
        slot = inner if slot is None else slot
        return remote(
            (k_ref, v_ref)[kind].at[:, lanes(h)], kv_row.at[slot, kind, :, lanes(h)],
            kvr_send.at[p, kind, h], kvr_recv.at[slot, kind, h], in_row(p), t,
        )

    def kv_col_copy(d, kind, h, slot=None):
        slot = 1 - d if slot is None else slot
        return remote(
            (k_ref, v_ref)[kind].at[:, lanes(h)], kv_col.at[slot, kind, :, lanes(h)],
            kvc_send.at[d, kind, h], kvc_recv.at[slot, kind, h], outer_of(d), t,
        )

    def group(kind, g):
        if g:
            return slice(middle * HD, (middle + 1) * HD)
        return slice(0, half * HD) if kind == "col" else slice((half + odd) * HD, cols)

    def q_row_copy(p, r, g, slot=None):
        slot = inner if slot is None else slot
        part = (rows(r), group("row", g))
        return remote(
            q_ref.at[part], q_row.at[(slot,) + part],
            qr_send.at[p, r, g], qr_recv.at[slot, r, g], in_row(p), t,
        )

    def q_col_copy(d, r, g, slot=None):
        slot = 1 - d if slot is None else slot
        part = (rows(r), group("col", g))
        return remote(
            q_ref.at[part], q_col.at[(slot,) + part],
            qc_send.at[d, r, g], qc_recv.at[slot, r, g], outer_of(d), t,
        )

    def o_row_copy(p, r, h, slot=None):
        slot = inner if slot is None else slot
        part = (rows(r), lanes(h))
        return remote(
            o_row.at[(p,) + part], got_row.at[(slot,) + part],
            or_send.at[p, r, h], or_recv.at[slot, r, h], in_row(p), t,
        )

    def o_col_copy(d, r, h, slot=None):
        slot = 1 - d if slot is None else slot
        part = (rows(r), lanes(h))
        return remote(
            o_col.at[(d,) + part], got_col.at[(slot,) + part],
            oc_send.at[d, r, h], oc_recv.at[slot, r, h], outer_of(d), t,
        )

    def lse_row_copy(p, r, slot=None):
        slot = inner if slot is None else slot
        return remote(
            lse_row.at[p, r], got_lse_row.at[slot, r],
            lr_send.at[p, r], lr_recv.at[slot, r], in_row(p), t,
        )

    def lse_col_copy(d, r, slot=None):
        slot = 1 - d if slot is None else slot
        return remote(
            lse_col.at[d, r], got_lse_col.at[slot, r],
            lc_send.at[d, r], lc_recv.at[slot, r], outer_of(d), t,
        )

    def weight_copy(jy):
        start = pl.multiple_of(tp_of(jy, 1 - core) * out_cols, out_cols)
        return remote(
            w_ref.at[:, pl.ds(start, out_cols)], w_peer.at[jy],
            wp_send.at[jy], wp_recv.at[jy], ctx, partner,
        )

    def att_copy(r):
        return remote(
            att.at[rows(r), :], att_peer.at[rows(r), :],
            att_send.at[r], att_recv.at[r], ctx, partner,
        )

    def chip_copy(jy, r, k):
        return remote(
            stage_y.at[jy - 1, r, k], recv_y.at[chips - jy - 1, r, k],
            y_send.at[jy - 1, r, k], y_recv.at[chips - jy - 1, r, k], ctx, tp_of(jy, core),
        )

    def out_copy(r, k):
        return pltpu.make_async_copy(
            final.at[r, k], out_ref.at[rows(r), k * width:(k + 1) * width], out_sem.at[r, k]
        )

    own = [
        pltpu.make_async_copy(q_ref, q_own, own_sem.at[0]),
        pltpu.make_async_copy(k_ref, kv_row.at[inner, K], own_sem.at[1]),
        pltpu.make_async_copy(v_ref, kv_row.at[inner, V], own_sem.at[2]),
    ]
    weights = []
    for jy in range(chips):
        start = pl.multiple_of(tp_of(jy, core) * out_cols, out_cols)
        weights.append(pltpu.make_async_copy(
            w_ref.at[:, pl.ds(start, out_cols)], w_own.at[jy], w_sem.at[jy]
        ))

    barrier = pltpu.get_barrier_semaphore()

    def greet(c, tt):
        pl.semaphore_signal(barrier, inc=1, device_id=(c, tt), device_id_type=MESH)

    each_peer(lambda p: greet(in_row(p), t))
    each_outer(lambda d: greet(outer_of(d), t))
    greet(ctx, partner)
    for jy in range(1, chips):
        greet(ctx, tp_of(jy, core))
    outer_count = inside(outer_of(DOWN)).astype(jnp.int32) + inside(outer_of(UP)).astype(jnp.int32)
    pl.semaphore_wait(barrier, reach - 1 + 1 + chips - 1 + outer_count)

    row_heads = list(range(half))
    col_heads = list(range(heads - 1, heads - 1 - half, -1))

    def by_core(which, fn):
        if odd:
            @pl.when(core == which)
            def _():
                fn()

    def start_queries(r):
        each_peer(lambda p: q_row_copy(p, r, 0).start())
        by_core(1, lambda: each_peer(lambda p: q_row_copy(p, r, 1).start()))
        each_outer(lambda d: q_col_copy(d, r, 0).start())
        by_core(0, lambda: each_outer(lambda d: q_col_copy(d, r, 1).start()))

    def start_row_keys(h):
        for kind in (K, V):
            each_peer(lambda p: kv_row_copy(p, kind, h).start())

    def start_col_keys(h):
        def go(d):
            for kind in (K, V):
                kv_col_copy(d, kind, h).start()
        each_outer(go)

    start_queries(0)
    for a, b in zip(row_heads, col_heads):
        start_row_keys(a)
        start_col_keys(b)
    by_core(0, lambda: start_row_keys(middle))
    by_core(1, lambda: start_col_keys(middle))
    for r in range(1, per):
        start_queries(r)
    for copy in own:
        copy.start()
    for jy in list(range(1, chips)) + [0]:
        weight_copy(jy).start()
    for copy in weights[1:] + weights[:1]:
        copy.start()

    for d in (DOWN, UP):
        @pl.when(jnp.logical_not(inside(outer_of(d))))
        def _(d=d):
            kv_col[d] = jnp.zeros(kv_col.shape[1:], kv_col.dtype)
            q_col[d] = jnp.zeros(q_col.shape[1:], q_col.dtype)
            got_col[d] = jnp.zeros(got_col.shape[1:], got_col.dtype)
            got_lse_col[d] = jnp.full(got_lse_col.shape[1:], NONE, jnp.float32)
    lse_row[...] = jnp.zeros_like(lse_row)
    lse_col[...] = jnp.zeros_like(lse_col)

    def bias_of(block, owner):
        owner_in = jnp.clip(owner, 0, count - 1)
        block_in = jnp.clip(block, 0, count * per - 1)
        parts = []
        for b in range(per):
            flag = jnp.where(inside(owner), mask_ref[block_in, owner_in * per + b], 0)
            value = jnp.where(flag > 0, jnp.float32(0.0), jnp.float32(NONE))
            parts.append(jnp.full((1, BLK), value, jnp.float32))
        return parts

    def scores_of(query, pieces):
        key = jnp.concatenate([piece[0] for piece in pieces], axis=0)
        return lax.dot_general(
            query, key, (((1,), (1,)), ((), ())), preferred_element_type=jnp.float32
        )

    def sums_of(weight, pieces):
        value = jnp.concatenate([piece[1] for piece in pieces], axis=0)
        ones = jnp.ones((value.shape[0], HD), jnp.bfloat16)
        return jnp.dot(
            weight, jnp.concatenate([value, ones], axis=1), preferred_element_type=jnp.float32
        )

    def partial(query, block, pieces):
        raw = scores_of(query, pieces)
        weight, tops = [], []
        for a in range(query.shape[0] // BLK):
            bias = jnp.concatenate(
                sum([bias_of(block + a, piece[2]) for piece in pieces], []), axis=1
            )
            scores = raw[rows(a)] + bias
            top = jnp.broadcast_to(jnp.max(scores, axis=1, keepdims=True), (BLK, HD))
            wide = jnp.concatenate([top] * (scores.shape[1] // HD), axis=1)
            weight.append(jnp.exp2((scores - wide) * factor).astype(jnp.bfloat16))
            tops.append(top * factor)
        return sums_of(jnp.concatenate(weight, axis=0), pieces), jnp.concatenate(tops, axis=0)

    def fade(before, after):
        scale = jnp.exp2(before - after)
        return jnp.concatenate([scale, scale], axis=1)

    def partial_row(query, block, h, low, high):
        def step(slot, carry):
            total, top = carry
            more, more_top = partial(query, block, [row_piece(slot, h)])
            best = jnp.maximum(top, more_top)
            return total * fade(top, best) + more * fade(more_top, best), best
        shape = (query.shape[0], HD)
        first = (jnp.zeros((shape[0], 2 * HD), jnp.float32), jnp.full(shape, -1e38, jnp.float32))
        return lax.fori_loop(low, high, step, first)

    def row_piece(slot, h):
        return kv_row[slot, K, :, lanes(h)], kv_row[slot, V, :, lanes(h)], in_row(slot)

    def col_piece(d, h):
        return kv_col[d, K, :, lanes(h)], kv_col[d, V, :, lanes(h)], outer_of(d)

    def keep(h, total, top):
        acc[h] = total
        peak[h] = top

    def own_row(h):
        query = q_own[:, lanes(h)]
        if reach == 2:
            pieces = [row_piece(inner, h), row_piece(1 - inner, h)]
            keep(h, *partial(query, ctx * per, pieces))
        else:
            keep(h, *partial_row(query, ctx * per, h, 0, reach))

    def own_col(h):
        pieces = [row_piece(inner, h), col_piece(DOWN, h), col_piece(UP, h)]
        keep(h, *partial(q_own[:, lanes(h)], ctx * per, pieces))

    def answer(total, top, o_ref, lse_ref, h):
        below = total[:, HD:]
        o_ref[...] = (total[:, :HD] * (1.0 / below)).astype(jnp.bfloat16)
        lse = top + jnp.log(below) * jnp.float32(math.log2(math.e))
        lse_ref[h:h + 1, :] = jnp.transpose(lse)[0:1, :]

    def answer_col(h, r):
        if reach == 2:
            far, close = 1 - inner, inner
            tasks = [
                (far, [row_piece(inner, h), row_piece(1 - inner, h)]),
                (close, [row_piece(inner, h)]),
            ]
            for d, pieces in tasks:
                total, top = partial(q_col[d, rows(r), lanes(h)], outer_of(d) * per + r, pieces)
                answer(total, top, o_col.at[d, rows(r), lanes(h)], lse_col.at[d, r], h)
        else:
            for d in (DOWN, UP):
                low, high = (0, inner + 1) if d == DOWN else (inner, reach)
                total, top = partial_row(
                    q_col[d, rows(r), lanes(h)], outer_of(d) * per + r, h, low, high
                )
                answer(total, top, o_col.at[d, rows(r), lanes(h)], lse_col.at[d, r], h)

    def answer_row(h, r):
        def one(p):
            d = (p > inner).astype(jnp.int32)
            pieces = [row_piece(inner, h), col_piece(d, h)]
            total, top = partial(q_row[p, rows(r), lanes(h)], in_row(p) * per + r, pieces)
            answer(total, top, o_row.at[p, rows(r), lanes(h)], lse_row.at[p, r], h)
        each_peer(one)

    def send_col(h, r):
        each_outer(lambda d: o_col_copy(d, r, h).start())

    def send_row(h, r):
        @pl.when(t >= 0)
        def _():
            each_peer(lambda p: o_row_copy(p, r, h).start())

    def send_lse(r):
        each_outer(lambda d: lse_col_copy(d, r).start())

        @pl.when(t >= 0)
        def _():
            each_peer(lambda p: lse_row_copy(p, r).start())

    def wait_row_keys(h):
        for kind in (K, V):
            each_peer(lambda p: kv_row_copy(p, kind, h, p).wait_recv())

    def wait_col_keys(h):
        def go(d):
            for kind in (K, V):
                kv_col_copy(d, kind, h, d).wait_recv()
        each_outer(go)

    def wait_queries(r):
        each_peer(lambda p: q_row_copy(p, r, 0, p).wait_recv())
        by_core(1, lambda: each_peer(lambda p: q_row_copy(p, r, 1, p).wait_recv()))
        each_outer(lambda d: q_col_copy(d, r, 0, d).wait_recv())
        by_core(0, lambda: each_outer(lambda d: q_col_copy(d, r, 1, d).wait_recv()))

    for copy in own:
        copy.wait()
    wait_queries(0)
    for a, b in zip(row_heads, col_heads):
        wait_row_keys(a)
        wait_col_keys(b)
        answer_col(a, 0)
        answer_row(b, 0)
        own_row(a)
        own_col(b)
        send_col(a, 0)
        send_row(b, 0)

    def middle_row():
        wait_row_keys(middle)
        answer_col(middle, 0)
        send_col(middle, 0)

    def middle_col():
        wait_col_keys(middle)
        answer_row(middle, 0)
        send_row(middle, 0)

    by_core(0, middle_row)
    by_core(1, middle_col)
    send_lse(0)
    by_core(0, lambda: own_row(middle))
    by_core(1, lambda: own_col(middle))

    for r in range(1, per):
        wait_queries(r)
        for a, b in zip(row_heads, col_heads):
            answer_col(a, r)
            answer_row(b, r)
        by_core(0, lambda: answer_col(middle, r))
        by_core(1, lambda: answer_row(middle, r))
        for a, b in zip(row_heads, col_heads):
            send_col(a, r)
            send_row(b, r)
        by_core(0, lambda: send_col(middle, r))
        by_core(1, lambda: send_row(middle, r))
        send_lse(r)

    def spread(row):
        return jnp.transpose(jnp.broadcast_to(row, (BLK, BLK)))

    def merge(h, r, parts):
        total, top = acc[h, rows(r), :], peak[h, rows(r), :]
        logs = [spread(lse) for _, lse in parts]
        best = functools.reduce(jnp.maximum, logs, top)
        scale = jnp.exp2(top - best)
        upper, below = total[:, :HD] * scale, total[:, HD:] * scale
        for (value, _), log in zip(parts, logs):
            weight = jnp.exp2(log - best)
            upper = upper + value.astype(jnp.float32) * weight
            below = below + weight
        return upper, below, best

    def finish(h, r, parts):
        upper, below, _ = merge(h, r, parts)
        att[rows(r), lanes(h)] = (upper * (1.0 / below)).astype(jnp.bfloat16)

    def finish_row(h, r):
        finish(h, r, [
            (got_col[d, rows(r), lanes(h)], got_lse_col[d, r, h:h + 1, :]) for d in (DOWN, UP)
        ])

    def finish_col(h, r):
        def part(p):
            return got_row[p, rows(r), lanes(h)], got_lse_row[p, r, h:h + 1, :]

        if reach == 2:
            finish(h, r, [part(1 - inner)])
        else:
            def fold(p):
                upper, below, best = merge(h, r, [part(p)])
                acc[h, rows(r), :] = jnp.concatenate([upper, below], axis=1)
                peak[h, rows(r), :] = best
            each_peer(fold)
            finish(h, r, [])

    def wait_answers(r):
        for h in row_heads:
            each_outer(lambda d: o_col_copy(d, r, h, d).wait_recv())
        for h in col_heads:
            each_peer(lambda p: o_row_copy(p, r, h, p).wait_recv())
        by_core(0, lambda: each_outer(lambda d: o_col_copy(d, r, middle, d).wait_recv()))
        by_core(1, lambda: each_peer(lambda p: o_row_copy(p, r, middle, p).wait_recv()))
        each_outer(lambda d: lse_col_copy(d, r, d).wait_recv())
        each_peer(lambda p: lse_row_copy(p, r, p).wait_recv())

    def project(jy, r, k):
        part = slice(k * width, (k + 1) * width)
        mine = jnp.dot(att[rows(r), :], w_own[jy, :, part], preferred_element_type=jnp.float32)
        other = jnp.dot(
            att_peer[rows(r), :], w_peer[jy, :, part], preferred_element_type=jnp.float32
        )
        return mine + other

    for copy in weights:
        copy.wait()
    for jy in range(chips):
        weight_copy(jy).wait_recv()
    for r in range(per):
        wait_answers(r)
        by_core(0, lambda: finish_row(middle, r))
        by_core(1, lambda: finish_col(middle, r))
        for a, b in zip(row_heads, col_heads):
            finish_row(a, r)
            finish_col(b, r)

        @pl.when(t >= 0)
        def _():
            att_copy(r).start()
        att_copy(r).wait_recv()
        for jy in range(1, chips):
            for k in range(chunks):
                stage_y[jy - 1, r, k] = project(jy, r, k).astype(jnp.bfloat16)

                @pl.when(t >= 0)
                def _():
                    chip_copy(jy, r, k).start()
        for k in range(chunks):
            near[r, k] = project(0, r, k)
    for r in range(per):
        for k in range(chunks):
            total = near[r, k]
            for jy in range(1, chips):
                chip_copy(chips - jy, r, k).wait_recv()
            for other in range(chips - 1):
                total = total + recv_y[other, r, k].astype(jnp.float32)
            final[r, k] = total.astype(jnp.bfloat16)

            @pl.when(t >= 0)
            def _():
                out_copy(r, k).start()

    for a, b in zip(row_heads, col_heads):
        for kind in (K, V):
            each_peer(lambda p: kv_row_copy(p, kind, a).wait_send())
            each_outer(lambda d: kv_col_copy(d, kind, b).wait_send())
        for r in range(per):
            each_outer(lambda d: o_col_copy(d, r, a).wait_send())
            each_peer(lambda p: o_row_copy(p, r, b).wait_send())

    def middle_row_end():
        for kind in (K, V):
            each_peer(lambda p: kv_row_copy(p, kind, middle).wait_send())
        for r in range(per):
            each_outer(lambda d: o_col_copy(d, r, middle).wait_send())
            each_outer(lambda d: q_col_copy(d, r, 1).wait_send())

    def middle_col_end():
        for kind in (K, V):
            each_outer(lambda d: kv_col_copy(d, kind, middle).wait_send())
        for r in range(per):
            each_peer(lambda p: o_row_copy(p, r, middle).wait_send())
            each_peer(lambda p: q_row_copy(p, r, 1).wait_send())

    by_core(0, middle_row_end)
    by_core(1, middle_col_end)
    for r in range(per):
        each_peer(lambda p: q_row_copy(p, r, 0).wait_send())
        each_outer(lambda d: q_col_copy(d, r, 0).wait_send())
        each_peer(lambda p: lse_row_copy(p, r).wait_send())
        each_outer(lambda d: lse_col_copy(d, r).wait_send())
        att_copy(r).wait_send()
    for jy in range(chips):
        weight_copy(jy).wait_send()
    for r in range(per):
        for k in range(chunks):
            for jy in range(1, chips):
                chip_copy(jy, r, k).wait_send()
            out_copy(r, k).wait()


def shards(count, tp_count, queries, keys, values, block_mask, w_out):
    tok, cols = queries.shape
    heads = cols // HD
    per = tok // BLK
    reach = count // 4
    chips = tp_count // 2
    depth, wide = w_out.shape
    out_cols = wide // tp_count
    chunks = max(1, out_cols // 256)
    width = out_cols // chunks
    bf16, f32 = jnp.bfloat16, jnp.float32
    dma = pltpu.SemaphoreType.DMA
    tall = -(-heads // 8) * 8
    return pl.pallas_call(
        functools.partial(kernel, reach, count, tp_count, chunks),
        out_shape=jax.ShapeDtypeStruct((tok, out_cols), bf16),
        in_specs=[
            pl.BlockSpec(memory_space=pltpu.SMEM),
            pl.BlockSpec(memory_space=pl.ANY),
            pl.BlockSpec(memory_space=pl.ANY),
            pl.BlockSpec(memory_space=pl.ANY),
            pl.BlockSpec(memory_space=pl.ANY),
        ],
        out_specs=pl.BlockSpec(memory_space=pl.ANY),
        scratch_shapes=[
            pltpu.VMEM((tok, cols), bf16),
            pltpu.VMEM((reach, 2, tok, cols), bf16),
            pltpu.VMEM((2, 2, tok, cols), bf16),
            pltpu.VMEM((reach, tok, cols), bf16),
            pltpu.VMEM((2, tok, cols), bf16),
            pltpu.VMEM((reach, tok, cols), bf16),
            pltpu.VMEM((2, tok, cols), bf16),
            pltpu.VMEM((reach, tok, cols), bf16),
            pltpu.VMEM((2, tok, cols), bf16),
            pltpu.VMEM((reach, per, tall, BLK), f32),
            pltpu.VMEM((2, per, tall, BLK), f32),
            pltpu.VMEM((reach, per, tall, BLK), f32),
            pltpu.VMEM((2, per, tall, BLK), f32),
            pltpu.VMEM((heads, tok, 2 * HD), f32),
            pltpu.VMEM((heads, tok, HD), f32),
            pltpu.VMEM((tok, cols), bf16),
            pltpu.VMEM((tok, cols), bf16),
            pltpu.VMEM((chips, depth, out_cols), bf16),
            pltpu.VMEM((chips, depth, out_cols), bf16),
            pltpu.VMEM((chips - 1, per, chunks, BLK, width), bf16),
            pltpu.VMEM((chips - 1, per, chunks, BLK, width), bf16),
            pltpu.VMEM((per, chunks, BLK, width), f32),
            pltpu.VMEM((per, chunks, BLK, width), bf16),
            dma((3,)),
            dma((chips,)),
            dma((chips,)),
            dma((chips,)),
            dma((reach, 2, heads)),
            dma((reach, 2, heads)),
            dma((2, 2, heads)),
            dma((2, 2, heads)),
            dma((reach, per, 2)),
            dma((reach, per, 2)),
            dma((2, per, 2)),
            dma((2, per, 2)),
            dma((reach, per, heads)),
            dma((reach, per, heads)),
            dma((2, per, heads)),
            dma((2, per, heads)),
            dma((reach, per)),
            dma((reach, per)),
            dma((2, per)),
            dma((2, per)),
            dma((per,)),
            dma((per,)),
            dma((chips - 1, per, chunks)),
            dma((chips - 1, per, chunks)),
            dma((per, chunks)),
        ],
        compiler_params=pltpu.CompilerParams(
            collective_id=0, has_side_effects=True, vmem_limit_bytes=60 * 1024 * 1024
        ),
    )(block_mask, queries, keys, values, w_out)


def solution(mesh):
    return jax.shard_map(
        functools.partial(shards, mesh.shape["ctx"], mesh.shape["tp"]),
        mesh=mesh,
        in_specs=(P("ctx", "tp"), P("ctx", "tp"), P("ctx", "tp"), P(), P("tp", None)),
        out_specs=P("ctx", "tp"),
        check_vma=False,
    )
```

time: 48.5 us -> 43.3 us (0.89)
  the two profiles are of different devices: /device:TPU:11 before, /device:TPU:1 now
where the time goes in v1:
time: 43.3 us; the launch traced here: 43.1 us
  Pallas kernels  41.1 us (95%)
  local copies, waits for them, and re-layouts  1.97 us (5%)
    pallas_call x1, Pallas kernels, shards(): pl.pallas_call(functools.partial(kernel, reach, count, tp_count, chunks),...  41.1 us
    unnamed x1, local copies, waits for them, and re-layouts  1.97 us

profile of v1, /device:TPU:1, one launch (start us, length us, event | category | flops | bytes accessed | tf_op | source)
XLA Modules:
  0.0 43.1 jit_solution(5759516773446221617)
XLA Ops:
  0.0 41.1 %shard_map.55 = bf16[256,1280]{1,0:T(8,128)(2,1)} custom-call(s32[16,16]{1,0:T(8,128)} %mask_ref.1, bf16[256,640]{1,0:T(8,128)(2,1)} %q_ref.1, bf16[256,640]{1,0:T(8,128)(2,1)} %k_ref.1, bf16[256,640]{1,0:T(8,128)(2,1)} %v_ref.1, bf16[640,5120]{1,0:T(8,128)(2,1)} %w_ref.1), custom_call_target="tpu_custom_call" | custom-call | tf_op jit(solution)/shard_map/pallas_call | solution.py:574
  41.2 2.0 %copy.7 = bf16[256,1280]{1,0:T(8,128)(2,1)} copy(bf16[256,1280]{1,0:T(8,128)(2,1)} %shard_map.55) | data formatting | bytes 1310720

commit v2 on v1

v2 whole, which is shorter than its diff:
```python
import contextlib
import functools
import math

import jax
import jax.numpy as jnp
from jax import lax
from jax.experimental import pallas as pl
from jax.experimental.pallas import tpu as pltpu
from jax.sharding import PartitionSpec as P

HD = 128
BLK = 128
MESH = pl.DeviceIdType.MESH
K, V = 0, 1
DOWN, UP = 0, 1
NONE = -1e30
phase = contextlib.nullcontext


def kernel(
    reach, count, tp_count, chunks,
    mask_hbm, q_ref, k_ref, v_ref, w_ref, out_ref,
    mask_ref, q_own, kv_row, kv_col, q_row, q_col, o_row, o_col, got_row, got_col,
    lse_row, lse_col, got_lse_row, got_lse_col, acc, peak, att, att_peer,
    w_own, w_peer, stage_y, recv_y, near,
    own_sem, w_sem, wp_send, wp_recv, kvr_send, kvr_recv, kvc_send, kvc_recv,
    qr_send, qr_recv, qc_send, qc_recv, or_send, or_recv, oc_send, oc_recv,
    lr_send, lr_recv, lc_send, lc_recv, att_send, att_recv, y_send, y_recv,
):
    tok, cols = q_own.shape
    heads = cols // HD
    per = tok // BLK
    chips = tp_count // 2
    out_cols = out_ref.shape[1]
    width = out_cols // chunks
    half = heads // 2
    odd = heads % 2
    middle = half
    ctx = lax.axis_index("ctx")
    t = lax.axis_index("tp")
    inner = lax.rem(ctx, reach)
    core = lax.rem(t, 2)
    chip = t // 2
    partner = chip * 2 + 1 - core
    factor = jnp.float32(HD ** (-0.5) * math.log2(math.e))

    def tp_of(jy, which):
        return lax.rem(chip + jy, chips) * 2 + which

    def each_peer(fn):
        if reach == 2:
            fn(1 - inner)
        elif reach > 2:
            def step(j, carry):
                fn(lax.rem(inner + j, reach))
                return carry
            lax.fori_loop(1, reach, step, 0)

    def in_row(p):
        return ctx - inner + p

    def outer_of(d):
        return ctx + (2 * d - 1) * reach

    def inside(c):
        return jnp.logical_and(c >= 0, c < count)

    def each_outer(fn):
        for d in (DOWN, UP):
            @pl.when(inside(outer_of(d)))
            def _(d=d):
                fn(d)

    def lanes(h):
        return slice(h * HD, (h + 1) * HD)

    def rows(r):
        return slice(r * BLK, (r + 1) * BLK)

    def remote(src, dst, send, recv, c, tt):
        return pltpu.make_async_remote_copy(
            src_ref=src, dst_ref=dst, send_sem=send, recv_sem=recv,
            device_id=(c, tt), device_id_type=MESH,
        )

    def turn(h):
        return h if h <= middle else heads - 1 - h

    def row_lanes(wide):
        return slice((half if wide else half + odd) * HD, cols)

    def col_lanes(wide):
        return slice(0, (half + odd if wide else half) * HD)

    def kv_row_copy(p, kind, h):
        return remote(
            (k_ref, v_ref)[kind].at[:, lanes(h)], kv_row.at[inner, kind, :, lanes(h)],
            kvr_send.at[p], kvr_recv.at[inner, turn(h)], in_row(p), t,
        )

    def kv_col_copy(d, kind, h):
        return remote(
            (k_ref, v_ref)[kind].at[:, lanes(h)], kv_col.at[1 - d, kind, :, lanes(h)],
            kvc_send.at[d], kvc_recv.at[1 - d, turn(h)], outer_of(d), t,
        )

    def q_row_copy(p, r, wide):
        part = (rows(r), row_lanes(wide))
        return remote(
            q_ref.at[part], q_row.at[(inner,) + part],
            qr_send.at[p], qr_recv.at[inner, r], in_row(p), t,
        )

    def q_col_copy(d, r, wide):
        part = (rows(r), col_lanes(wide))
        return remote(
            q_ref.at[part], q_col.at[(1 - d,) + part],
            qc_send.at[d], qc_recv.at[1 - d, r], outer_of(d), t,
        )

    def o_row_copy(p, r, h):
        part = (rows(r), lanes(h))
        return remote(
            o_row.at[(p,) + part], got_row.at[(inner,) + part],
            or_send.at[p], or_recv.at[inner, r], in_row(p), t,
        )

    def o_col_copy(d, r, h):
        part = (rows(r), lanes(h))
        return remote(
            o_col.at[(d,) + part], got_col.at[(1 - d,) + part],
            oc_send.at[d], oc_recv.at[1 - d, r], outer_of(d), t,
        )

    def lse_row_copy(p, r):
        return remote(
            lse_row.at[p, r], got_lse_row.at[inner, r],
            lr_send.at[p], lr_recv.at[inner, r], in_row(p), t,
        )

    def lse_col_copy(d, r):
        return remote(
            lse_col.at[d, r], got_lse_col.at[1 - d, r],
            lc_send.at[d], lc_recv.at[1 - d, r], outer_of(d), t,
        )

    def arrived(ref, sem):
        remote(ref, ref, wp_send.at[0], sem, ctx, partner).wait_recv()

    def sent(ref, sem):
        remote(ref, ref, sem, wp_recv.at[0], ctx, partner).wait_send()

    def weight_copy(jy):
        start = pl.multiple_of(tp_of(jy, 1 - core) * out_cols, out_cols)
        return remote(
            w_ref.at[:, pl.ds(start, out_cols)], w_peer.at[jy],
            wp_send.at[0], wp_recv.at[jy], ctx, partner,
        )

    def att_copy(r):
        return remote(
            att.at[rows(r), :], att_peer.at[rows(r), :],
            att_send.at[0], att_recv.at[r], ctx, partner,
        )

    def chip_copy(jy, r, k):
        return remote(
            stage_y.at[jy - 1, r, k], recv_y.at[chips - jy - 1, r, k],
            y_send.at[0], y_recv.at[chips - jy - 1, r, k], ctx, tp_of(jy, core),
        )

    own = [
        pltpu.make_async_copy(mask_hbm, mask_ref, own_sem.at[3]),
        pltpu.make_async_copy(q_ref, q_own, own_sem.at[0]),
        pltpu.make_async_copy(k_ref, kv_row.at[inner, K], own_sem.at[1]),
        pltpu.make_async_copy(v_ref, kv_row.at[inner, V], own_sem.at[2]),
    ]
    weights = []
    for jy in range(chips):
        start = pl.multiple_of(tp_of(jy, core) * out_cols, out_cols)
        weights.append(pltpu.make_async_copy(
            w_ref.at[:, pl.ds(start, out_cols)], w_own.at[jy], w_sem.at[jy]
        ))

    for copy in own:
        copy.start()
    barrier = pltpu.get_barrier_semaphore()

    def greet(c, tt):
        pl.semaphore_signal(barrier, inc=1, device_id=(c, tt), device_id_type=MESH)

    with phase("bar"):
        each_peer(lambda p: greet(in_row(p), t))
        each_outer(lambda d: greet(outer_of(d), t))
        greet(ctx, partner)
        for jy in range(1, chips):
            greet(ctx, tp_of(jy, core))
        outer_count = inside(outer_of(DOWN)).astype(jnp.int32) + inside(outer_of(UP)).astype(jnp.int32)
        pl.semaphore_wait(barrier, reach - 1 + 1 + chips - 1 + outer_count)

    row_heads = list(range(half))
    col_heads = list(range(heads - 1, heads - 1 - half, -1))

    def by_core(which, fn):
        if odd:
            @pl.when(core == which)
            def _():
                fn()

    def each_core(fn):
        if odd:
            for which in (0, 1):
                by_core(which, lambda which=which: fn(which == 1, which == 0))
        else:
            fn(False, False)

    def start_queries(r):
        def go(row_wide, col_wide):
            each_peer(lambda p: q_row_copy(p, r, row_wide).start())
            each_outer(lambda d: q_col_copy(d, r, col_wide).start())
        each_core(go)

    def start_row_keys(h):
        for kind in (K, V):
            each_peer(lambda p: kv_row_copy(p, kind, h).start())

    def start_col_keys(h):
        def go(d):
            for kind in (K, V):
                kv_col_copy(d, kind, h).start()
        each_outer(go)

    with phase("starts"):
        start_queries(0)
        for a, b in zip(row_heads, col_heads):
            start_row_keys(a)
            start_col_keys(b)
        by_core(0, lambda: start_row_keys(middle))
        by_core(1, lambda: start_col_keys(middle))
        for r in range(1, per):
            start_queries(r)

    for d in (DOWN, UP):
        @pl.when(jnp.logical_not(inside(outer_of(d))))
        def _(d=d):
            kv_col[d] = jnp.zeros(kv_col.shape[1:], kv_col.dtype)
            q_col[d] = jnp.zeros(q_col.shape[1:], q_col.dtype)
            got_col[d] = jnp.zeros(got_col.shape[1:], got_col.dtype)
            got_lse_col[d] = jnp.full(got_lse_col.shape[1:], NONE, jnp.float32)
    lse_row[...] = jnp.zeros_like(lse_row)
    lse_col[...] = jnp.zeros_like(lse_col)

    def bias_of(block, owner):
        owner_in = jnp.clip(owner, 0, count - 1)
        block_in = jnp.clip(block, 0, count * per - 1)
        parts = []
        for b in range(per):
            flag = jnp.where(inside(owner), mask_ref[block_in, owner_in * per + b], 0)
            value = jnp.where(flag > 0, jnp.float32(0.0), jnp.float32(NONE))
            parts.append(jnp.full((1, BLK), value, jnp.float32))
        return parts

    def scores_of(query, pieces):
        key = jnp.concatenate([piece[0] for piece in pieces], axis=0)
        return lax.dot_general(
            query, key, (((1,), (1,)), ((), ())), preferred_element_type=jnp.float32
        )

    def sums_of(weight, pieces):
        value = jnp.concatenate([piece[1] for piece in pieces], axis=0)
        ones = jnp.ones((value.shape[0], HD), jnp.bfloat16)
        return jnp.dot(
            weight, jnp.concatenate([value, ones], axis=1), preferred_element_type=jnp.float32
        )

    def partial(query, block, pieces):
        raw = scores_of(query, pieces)
        weight, tops = [], []
        for a in range(query.shape[0] // BLK):
            bias = jnp.concatenate(
                sum([bias_of(block + a, piece[2]) for piece in pieces], []), axis=1
            )
            scores = raw[rows(a)] + bias
            top = jnp.broadcast_to(jnp.max(scores, axis=1, keepdims=True), (BLK, HD))
            wide = jnp.concatenate([top] * (scores.shape[1] // HD), axis=1)
            weight.append(jnp.exp2((scores - wide) * factor).astype(jnp.bfloat16))
            tops.append(top * factor)
        return sums_of(jnp.concatenate(weight, axis=0), pieces), jnp.concatenate(tops, axis=0)

    def fade(before, after):
        scale = jnp.exp2(before - after)
        return jnp.concatenate([scale, scale], axis=1)

    def partial_row(query, block, h, low, high):
        def step(slot, carry):
            total, top = carry
            more, more_top = partial(query, block, [row_piece(slot, h)])
            best = jnp.maximum(top, more_top)
            return total * fade(top, best) + more * fade(more_top, best), best
        shape = (query.shape[0], HD)
        first = (jnp.zeros((shape[0], 2 * HD), jnp.float32), jnp.full(shape, -1e38, jnp.float32))
        return lax.fori_loop(low, high, step, first)

    def row_piece(slot, h):
        return kv_row[slot, K, :, lanes(h)], kv_row[slot, V, :, lanes(h)], in_row(slot)

    def col_piece(d, h):
        return kv_col[d, K, :, lanes(h)], kv_col[d, V, :, lanes(h)], outer_of(d)

    def keep(h, total, top):
        acc[h] = total
        peak[h] = top

    def own_row(h):
        query = q_own[:, lanes(h)]
        if reach == 2:
            pieces = [row_piece(inner, h), row_piece(1 - inner, h)]
            keep(h, *partial(query, ctx * per, pieces))
        else:
            keep(h, *partial_row(query, ctx * per, h, 0, reach))

    def own_col(h):
        pieces = [row_piece(inner, h), col_piece(DOWN, h), col_piece(UP, h)]
        keep(h, *partial(q_own[:, lanes(h)], ctx * per, pieces))

    def answer(total, top, o_ref, lse_ref, h):
        below = total[:, HD:]
        o_ref[...] = (total[:, :HD] * (1.0 / below)).astype(jnp.bfloat16)
        lse = top + jnp.log(below) * jnp.float32(math.log2(math.e))
        lse_ref[h:h + 1, :] = jnp.transpose(lse)[0:1, :]

    def answer_col(h, r):
        if reach == 2:
            far, close = 1 - inner, inner
            tasks = [
                (far, [row_piece(inner, h), row_piece(1 - inner, h)]),
                (close, [row_piece(inner, h)]),
            ]
            for d, pieces in tasks:
                total, top = partial(q_col[d, rows(r), lanes(h)], outer_of(d) * per + r, pieces)
                answer(total, top, o_col.at[d, rows(r), lanes(h)], lse_col.at[d, r], h)
        else:
            for d in (DOWN, UP):
                low, high = (0, inner + 1) if d == DOWN else (inner, reach)
                total, top = partial_row(
                    q_col[d, rows(r), lanes(h)], outer_of(d) * per + r, h, low, high
                )
                answer(total, top, o_col.at[d, rows(r), lanes(h)], lse_col.at[d, r], h)

    def answer_row(h, r):
        def one(p):
            d = (p > inner).astype(jnp.int32)
            pieces = [row_piece(inner, h), col_piece(d, h)]
            total, top = partial(q_row[p, rows(r), lanes(h)], in_row(p) * per + r, pieces)
            answer(total, top, o_row.at[p, rows(r), lanes(h)], lse_row.at[p, r], h)
        each_peer(one)

    def send_col(h, r):
        each_outer(lambda d: o_col_copy(d, r, h).start())

    def send_row(h, r):
        @pl.when(t >= 0)
        def _():
            each_peer(lambda p: o_row_copy(p, r, h).start())

    def send_lse(r):
        each_outer(lambda d: lse_col_copy(d, r).start())

        @pl.when(t >= 0)
        def _():
            each_peer(lambda p: lse_row_copy(p, r).start())

    def wait_row_keys(h):
        each_peer(lambda p: arrived(kv_row.at[p, :, :, lanes(h)], kvr_recv.at[p, turn(h)]))

    def wait_col_keys(h):
        each_outer(lambda d: arrived(kv_col.at[d, :, :, lanes(h)], kvc_recv.at[d, turn(h)]))

    def wait_queries(r):
        def go(row_wide, col_wide):
            each_peer(lambda p: arrived(
                q_row.at[p, rows(r), row_lanes(row_wide)], qr_recv.at[p, r]))
            each_outer(lambda d: arrived(
                q_col.at[d, rows(r), col_lanes(col_wide)], qc_recv.at[d, r]))
        each_core(go)

    with phase("waitown"):
        for copy in own:
            copy.wait()
    with phase("waitq"):
        wait_queries(0)
    for jy in list(range(1, chips)) + [0]:
        weight_copy(jy).start()
    for copy in weights[1:] + weights[:1]:
        copy.start()
    for a, b in zip(row_heads, col_heads):
        with phase("waitkv"):
            wait_row_keys(a)
            wait_col_keys(b)
        with phase("step"):
            answer_col(a, 0)
            answer_row(b, 0)
            own_row(a)
            own_col(b)
            send_col(a, 0)
            send_row(b, 0)

    def middle_row():
        with phase("mwaitkv"):
            wait_row_keys(middle)
        answer_col(middle, 0)
        send_col(middle, 0)

    def middle_col():
        with phase("mwaitkv"):
            wait_col_keys(middle)
        answer_row(middle, 0)
        send_row(middle, 0)

    with phase("mid"):
        by_core(0, middle_row)
        by_core(1, middle_col)
        send_lse(0)
    with phase("ownmid"):
        by_core(0, lambda: own_row(middle))
        by_core(1, lambda: own_col(middle))

    for r in range(1, per):
        with phase("waitq1"):
            wait_queries(r)
        with phase("answer1"):
            for a, b in zip(row_heads, col_heads):
                answer_col(a, r)
                answer_row(b, r)
            by_core(0, lambda: answer_col(middle, r))
            by_core(1, lambda: answer_row(middle, r))
            for a, b in zip(row_heads, col_heads):
                send_col(a, r)
                send_row(b, r)
            by_core(0, lambda: send_col(middle, r))
            by_core(1, lambda: send_row(middle, r))
            send_lse(r)

    def spread(row):
        return jnp.transpose(jnp.broadcast_to(row, (BLK, BLK)))

    def merge(h, r, parts):
        total, top = acc[h, rows(r), :], peak[h, rows(r), :]
        logs = [spread(lse) for _, lse in parts]
        best = functools.reduce(jnp.maximum, logs, top)
        scale = jnp.exp2(top - best)
        upper, below = total[:, :HD] * scale, total[:, HD:] * scale
        for (value, _), log in zip(parts, logs):
            weight = jnp.exp2(log - best)
            upper = upper + value.astype(jnp.float32) * weight
            below = below + weight
        return upper, below, best

    def finish(h, r, parts):
        upper, below, _ = merge(h, r, parts)
        att[rows(r), lanes(h)] = (upper * (1.0 / below)).astype(jnp.bfloat16)

    def finish_row(h, r):
        finish(h, r, [
            (got_col[d, rows(r), lanes(h)], got_lse_col[d, r, h:h + 1, :]) for d in (DOWN, UP)
        ])

    def finish_col(h, r):
        def part(p):
            return got_row[p, rows(r), lanes(h)], got_lse_row[p, r, h:h + 1, :]

        if reach == 2:
            finish(h, r, [part(1 - inner)])
        else:
            def fold(p):
                upper, below, best = merge(h, r, [part(p)])
                acc[h, rows(r), :] = jnp.concatenate([upper, below], axis=1)
                peak[h, rows(r), :] = best
            each_peer(fold)
            finish(h, r, [])

    def wait_answers(r):
        def go(row_wide, col_wide):
            each_peer(lambda p: arrived(
                got_row.at[p, rows(r), row_lanes(row_wide)], or_recv.at[p, r]))
            each_outer(lambda d: arrived(
                got_col.at[d, rows(r), col_lanes(col_wide)], oc_recv.at[d, r]))
        each_core(go)
        each_outer(lambda d: arrived(got_lse_col.at[d, r], lc_recv.at[d, r]))
        each_peer(lambda p: arrived(got_lse_row.at[p, r], lr_recv.at[p, r]))

    def project(jy, r, k):
        part = slice(k * width, (k + 1) * width)
        mine = jnp.dot(att[rows(r), :], w_own[jy, :, part], preferred_element_type=jnp.float32)
        other = jnp.dot(
            att_peer[rows(r), :], w_peer[jy, :, part], preferred_element_type=jnp.float32
        )
        return mine + other

    with phase("waitw"):
        for copy in weights:
            copy.wait()
        for jy in range(chips):
            weight_copy(jy).wait_recv()
    for r in range(per):
        with phase("waitans"):
            wait_answers(r)
        with phase("finish"):
            by_core(0, lambda: finish_row(middle, r))
            by_core(1, lambda: finish_col(middle, r))
            for a, b in zip(row_heads, col_heads):
                finish_row(a, r)
                finish_col(b, r)

            @pl.when(t >= 0)
            def _():
                att_copy(r).start()
        with phase("waitatt"):
            att_copy(r).wait_recv()
        with phase("far"):
            for jy in range(1, chips):
                for k in range(chunks):
                    stage_y[jy - 1, r, k] = project(jy, r, k).astype(jnp.bfloat16)

                    @pl.when(t >= 0)
                    def _():
                        chip_copy(jy, r, k).start()
        with phase("near"):
            for k in range(chunks):
                near[r, k] = project(0, r, k)
    with phase("final"):
        for r in range(per):
            for k in range(chunks):
                total = near[r, k]
                for jy in range(1, chips):
                    chip_copy(chips - jy, r, k).wait_recv()
                for other in range(chips - 1):
                    total = total + recv_y[other, r, k].astype(jnp.float32)
                out_ref[rows(r), k * width:(k + 1) * width] = total.astype(jnp.bfloat16)

    with phase("tail"):
        def go(row_wide, col_wide):
            def row_sent(p):
                sent(kv_row.at[p, :, :, col_lanes(col_wide)], kvr_send.at[p])
                sent(q_row.at[p, :, row_lanes(row_wide)], qr_send.at[p])
                sent(o_row.at[p, :, row_lanes(row_wide)], or_send.at[p])
                sent(lse_row.at[p], lr_send.at[p])

            def col_sent(d):
                sent(kv_col.at[d, :, :, row_lanes(row_wide)], kvc_send.at[d])
                sent(q_col.at[d, :, col_lanes(col_wide)], qc_send.at[d])
                sent(o_col.at[d, :, col_lanes(col_wide)], oc_send.at[d])
                sent(lse_col.at[d], lc_send.at[d])

            each_peer(row_sent)
            each_outer(col_sent)
        each_core(go)
        sent(att, att_send.at[0])
        sent(w_peer, wp_send.at[0])
        sent(stage_y, y_send.at[0])


def shards(count, tp_count, queries, keys, values, block_mask, w_out):
    tok, cols = queries.shape
    heads = cols // HD
    per = tok // BLK
    reach = count // 4
    chips = tp_count // 2
    depth, wide = w_out.shape
    out_cols = wide // tp_count
    chunks = max(1, out_cols // 256)
    width = out_cols // chunks
    bf16, f32 = jnp.bfloat16, jnp.float32
    dma = pltpu.SemaphoreType.DMA
    tall = -(-heads // 8) * 8
    turns = heads // 2 + heads % 2
    return pl.pallas_call(
        functools.partial(kernel, reach, count, tp_count, chunks),
        out_shape=pltpu.VMEM((tok, out_cols), bf16),
        in_specs=[
            pl.BlockSpec(memory_space=pltpu.HBM),
            pl.BlockSpec(memory_space=pltpu.HBM),
            pl.BlockSpec(memory_space=pltpu.HBM),
            pl.BlockSpec(memory_space=pltpu.HBM),
            pl.BlockSpec(memory_space=pltpu.HBM),
        ],
        out_specs=pl.BlockSpec(memory_space=pltpu.VMEM),
        scratch_shapes=[
            pltpu.SMEM(block_mask.shape, block_mask.dtype),
            pltpu.VMEM((tok, cols), bf16),
            pltpu.VMEM((reach, 2, tok, cols), bf16),
            pltpu.VMEM((2, 2, tok, cols), bf16),
            pltpu.VMEM((reach, tok, cols), bf16),
            pltpu.VMEM((2, tok, cols), bf16),
            pltpu.VMEM((reach, tok, cols), bf16),
            pltpu.VMEM((2, tok, cols), bf16),
            pltpu.VMEM((reach, tok, cols), bf16),
            pltpu.VMEM((2, tok, cols), bf16),
            pltpu.VMEM((reach, per, tall, BLK), f32),
            pltpu.VMEM((2, per, tall, BLK), f32),
            pltpu.VMEM((reach, per, tall, BLK), f32),
            pltpu.VMEM((2, per, tall, BLK), f32),
            pltpu.VMEM((heads, tok, 2 * HD), f32),
            pltpu.VMEM((heads, tok, HD), f32),
            pltpu.VMEM((tok, cols), bf16),
            pltpu.VMEM((tok, cols), bf16),
            pltpu.VMEM((chips, depth, out_cols), bf16),
            pltpu.VMEM((chips, depth, out_cols), bf16),
            pltpu.VMEM((chips - 1, per, chunks, BLK, width), bf16),
            pltpu.VMEM((chips - 1, per, chunks, BLK, width), bf16),
            pltpu.VMEM((per, chunks, BLK, width), f32),
            dma((4,)),
            dma((chips,)),
            dma((1,)),
            dma((chips,)),
            dma((reach,)),
            dma((reach, turns)),
            dma((2,)),
            dma((2, turns)),
            dma((reach,)),
            dma((reach, per)),
            dma((2,)),
            dma((2, per)),
            dma((reach,)),
            dma((reach, per)),
            dma((2,)),
            dma((2, per)),
            dma((reach,)),
            dma((reach, per)),
            dma((2,)),
            dma((2, per)),
            dma((1,)),
            dma((per,)),
            dma((1,)),
            dma((chips - 1, per, chunks)),
        ],
        compiler_params=pltpu.CompilerParams(
            collective_id=0, has_side_effects=True, vmem_limit_bytes=56 * 1024 * 1024
        ),
    )(block_mask, queries, keys, values, w_out)


def solution(mesh):
    return jax.shard_map(
        functools.partial(shards, mesh.shape["ctx"], mesh.shape["tp"]),
        mesh=mesh,
        in_specs=(P("ctx", "tp"), P("ctx", "tp"), P("ctx", "tp"), P(), P("tp", None)),
        out_specs=P("ctx", "tp"),
        check_vma=False,
    )
```

time: 43.3 us -> 39.2 us (0.905)
  Pallas kernels: 41.1 us -> 38.2 us
  local copies, waits for them, and re-layouts: 1.97 us -> 0.84 us
    pallas_call x1, Pallas kernels: 41.1 us -> 38.2 us  [shards(): pl.pallas_call(functools.partial(kernel, reach, count, tp_count, chunks),...]
    unnamed x1, local copies, waits for them, and re-layouts: 1.97 us -> 0.84 us
where the time goes in v2:
time: 39.2 us; the launch traced here: 39 us
  Pallas kernels  38.2 us (97%)
  local copies, waits for them, and re-layouts  0.84 us (2%)
    pallas_call x1, Pallas kernels, shards(): pl.pallas_call(functools.partial(kernel, reach, count, tp_count, chunks),...  38.2 us
    unnamed x1, local copies, waits for them, and re-layouts  0.84 us

profile of v2, /device:TPU:1, one launch (start us, length us, event | category | flops | bytes accessed | tf_op | source)
XLA Modules:
  0.0 39.0 jit_solution(12563046379611121309)
XLA Ops:
  0.0 38.2 %shard_map.55 = bf16[256,1280]{1,0:T(8,128)(2,1)S(1)} custom-call(s32[16,16]{1,0:T(8,128)} %mask_hbm.1, bf16[256,640]{1,0:T(8,128)(2,1)} %q_ref.1, bf16[256,640]{1,0:T(8,128)(2,1)} %k_ref.1, bf16[256,640]{1,0:T(8,128)(2,1)} %v_ref.1, bf16[640,5120]{1,0:T(8,128)(2,1)} %w_ref.1), custom_call_target="tpu_custom_call" | custom-call | tf_op jit(solution)/shard_map/pallas_call | solution.py:578
  38.2 0.8 %copy.7 = bf16[256,1280]{1,0:T(8,128)(2,1)} copy(bf16[256,1280]{1,0:T(8,128)(2,1)S(1)} %shard_map.55) | data formatting | bytes 1310720
